TPU v7x, 32 devices: a whole 2x2x4 slice. The times are simulated.
32 devices in a mesh: groups: 2 (over y), edge: 4 (over z), expert: 2 (over x), sys: 2 (over core).
Axes of the slice: x: 2, y: 2, z: 4, core: 2. Of those that a mesh axis runs over, the one named last changes fastest.
Arguments:
- edge_inputs: bfloat16 [8, 1792, 1280], P(('groups', 'expert', 'sys'), 'edge'), parts along dimension 0, may hold values from -6 to 6
- out_grad: bfloat16 [8, 1792, 1152], P(('groups', 'expert', 'sys'), 'edge'), parts along dimension 0, may hold values from -6 to 6
- expert_weights: bfloat16 [32, 1280, 1152], P('expert', 'edge'), may hold values from -0.15625 to 0.15625
- coef_table: float32 [16, 32], replicated, may hold values from 0.05 to 0.5
- system_kind: int32 [8], P('groups'), parts along dimension 0, may hold values from 0 to 15
- edge_counts: int32 [8], P('groups'), parts along dimension 0, may hold values from 896 to 1792, as said below
Outputs:
- input_grad: bfloat16 [8, 1792, 1280], P(('groups', 'expert', 'sys'), 'edge'), parts along dimension 0
- weight_grad: bfloat16 [64, 1280, 1152], P(('groups', 'expert'), 'edge'), parts along dimension 0
There are 2 independent parts, one for each index of `groups`. A program takes and returns all parts, laid end to end along the dimension named above; an argument that names none is the same for every part. Nothing has to cross between parts.
Inputs may be any that keep to these rules, and one draw needn't show every extreme that they name: `edge_counts`: the live edges of a system are its first ones. One system has all 1792 slots live and another exactly half of them.
All inputs are finite; a program needn't handle non-finite values.
Results may differ from a plain program's by a relative error of at most 0.018.
Values may be sent and summed in bfloat16 or wider, within the bound.
No kernel may reach another device: no remote copies, remote signals or barrier semaphores. Data moves between devices by JAX's collectives and lax.ppermute only.
A program may use at most 128 MiB of HBM per device.

v0:
```python
import math
import jax
import jax.numpy as jnp
from jax import lax
from jax.sharding import PartitionSpec as P


def body(edge_inputs, out_grad, expert_weights, coef_table, system_kind, edge_counts):
    highest = lax.Precision.HIGHEST
    edge_size = lax.axis_size("edge")
    expert_size = lax.axis_size("expert")
    sys_size = lax.axis_size("sys")
    edge_at = lax.axis_index("edge")
    expert_at = lax.axis_index("expert")
    sys_at = lax.axis_index("sys")
    systems = system_kind.shape[0]
    kinds = coef_table.shape[0]
    exp_local = expert_weights.shape[0]
    row_count = expert_weights.shape[1]
    width_out = expert_weights.shape[2]
    edge_rows = out_grad.shape[1]
    onehot = (system_kind[:, None] == jnp.arange(kinds, dtype=jnp.int32)[None, :]).astype(
        jnp.float32
    )
    coeffs = jnp.dot(onehot, coef_table, precision=highest)
    own_system = expert_at * sys_size + sys_at
    picked = jnp.arange(systems, dtype=jnp.int32) == own_system
    own_count = jnp.sum(jnp.where(picked, edge_counts, 0))
    positions = edge_at * edge_rows + jnp.arange(edge_rows, dtype=jnp.int32)
    masked_grad = jnp.where(
        (positions < own_count)[:, None], out_grad[0], jnp.zeros((), jnp.bfloat16)
    )
    features = edge_inputs[0]
    by_block = coeffs.reshape(expert_size, sys_size, -1)
    same_sys = lax.dynamic_slice_in_dim(by_block, sys_at, 1, 1)[:, 0, :]
    own_coeffs = lax.dynamic_slice_in_dim(same_sys, expert_at * exp_local, exp_local, 1)
    partials = jnp.sum(
        own_coeffs[:, :, None, None] * expert_weights.astype(jnp.float32)[None], axis=1
    ).astype(jnp.bfloat16)
    merged_rows = jnp.sum(
        lax.all_to_all(partials, "expert", split_axis=0, concat_axis=0, tiled=True).astype(
            jnp.float32
        ),
        axis=0,
    ).astype(jnp.bfloat16)
    product = lax.dot_general(
        masked_grad,
        lax.all_gather(merged_rows, "edge", axis=0, tiled=True),
        (((1,), (1,)), ((), ())),
        preferred_element_type=jnp.float32,
    )
    input_grad = product.astype(jnp.bfloat16)
    system_rows = lax.psum_scatter(
        lax.dot_general(
            features, masked_grad, (((0,), (0,)), ((), ())), preferred_element_type=jnp.float32
        ).astype(jnp.bfloat16),
        "edge",
        scatter_dimension=0,
        tiled=True,
    )
    local_coeffs = lax.dynamic_slice_in_dim(coeffs, expert_at * exp_local, exp_local, 1).T
    block_rows = lax.all_gather(system_rows[None], ("expert", "sys"), axis=0, tiled=True)
    span_rows = block_rows.shape[0]
    flat_rows = block_rows.reshape(span_rows, -1).astype(jnp.float32)
    folded = jnp.dot(local_coeffs, flat_rows, precision=highest)
    scale_factor = 1.0 / math.sqrt(edge_rows * edge_size)
    weight_grad = (
        (folded * scale_factor).reshape(exp_local, row_count, width_out).astype(jnp.bfloat16)
    )
    return (input_grad[None], weight_grad)


def solution(mesh):
    return jax.shard_map(
        body,
        mesh=mesh,
        in_specs=(
            P(("groups", "expert", "sys"), "edge", None),
            P(("groups", "expert", "sys"), "edge", None),
            P("expert", "edge", None),
            P(),
            P("groups"),
            P("groups"),
        ),
        out_specs=(
            P(("groups", "expert", "sys"), "edge", None),
            P(("groups", "expert"), "edge", None),
        ),
        check_vma=False,
    )
```

profile of v0, /device:TPU:0, one launch (start us, length us, event | category | flops | bytes accessed | tf_op | source)
XLA Modules:
  0.0 198.3 jit_solution(15670721173112743282)
XLA Ops:
  7.2 0.0 copy-start
  7.2 0.0 reduce-scatter.4.cloned.1.call-start
  7.2 1.4 fusion.13
  8.6 0.7 add_compare_fusion
  9.3 0.0 copy-done
  9.3 4.7 %fusion.1 = bf16[1280,1152]{0,1:T(8,128)(2,1)} fusion(bf16[1,448,1280]{2,1,0:T(8,128)(2,1)S(1)} %copy-done, bf16[1,448,1152]{2,1,0:T(8,128)(2,1)} %param.7, pred[448]{0:T(512)(128)(4,1)S(1)} %add_compare_fusion), kind=kOutput, calls=%fused_computation.4 | convolution fusion | flops 1323196416 | bytes 5128640 | tf_op jit(solution)/shard_map/dot_general | solution.py:54
  13.9 5.4 %copy.11 = bf16[1280,1152]{1,0:T(8,128)(2,1)} copy(bf16[1280,1152]{0,1:T(8,128)(2,1)} %fusion.1) | data formatting | bytes 5898240
  19.4 0.0 reduce-scatter.4.cloned.1.call-update
  19.4 0.0 all-gather.4.cloned.1.call-start
  19.5 0.0 copy-start.3
  19.5 0.0 copy-start.4
  19.5 13.6 %convert_element_type.25 = f32[16,320,1152]{2,1,0:T(8,128)} convert(bf16[16,320,1152]{2,1,0:T(8,128)(2,1)} %param.8) | non-fusion elementwise | flops 5898240 | bytes 35389440 | tf_op jit(solution)/shard_map/convert_element_type | solution.py:38
  33.1 0.0 copy-done.3
  33.1 0.0 copy-done.4
  33.1 0.2 fusion.11
  33.3 0.1 constant_dynamic-slice_fusion
  33.4 13.5 %multiply_reduce_fusion = bf16[2,320,1152]{2,1,0:T(8,128)(2,1)S(1)} fusion(f32[16,320,1152]{2,1,0:T(8,128)} %convert_element_type.25, f32[2,16]{1,0:T(2,128)S(1)} %bitcast.24), kind=kLoop, calls=%fused_computation.2 | loop fusion | flops 22855680 | bytes 25067648 | tf_op jit(solution)/shard_map/reduce_sum | solution.py:37
  46.8 0.0 copy-start.2
  46.9 22.3 %all_to_all.5 = bf16[2,320,1152]{2,1,0:T(8,128)(2,1)S(1)} all-to-all(bf16[2,320,1152]{2,1,0:T(8,128)(2,1)S(1)} %multiply_reduce_fusion), channel_id=1, replica_groups=mesh['groups'=2,'edge'=4,'expert'=2,'sys'=2] {'expert'}, dimensions={0} | all-to-all | bytes 2949120 | tf_op jit(solution)/shard_map/all_to_all | solution.py:41
  69.2 1.3 reduce_sum.32
  70.5 0.0 all-gather.4.cloned.1.call-update
  70.5 0.0 all-gather.6.cloned.1.call-start
  70.6 9.0 %reduce-scatter.4.cloned.1.call-done = bf16[320,1152]{1,0:T(8,128)(2,1)} async-done(((bf16[1280,1152]{1,0:T(8,128)(2,1)}), bf16[320,1152]{1,0:T(8,128)(2,1)}) %reduce-scatter.4.cloned.1.call-update) | async-done | bytes 737296 | tf_op jit(solution)/shard_map/reduce_scatter | solution.py:53
  79.6 0.0 all-gather.6.cloned.1.call-update
  79.7 62.1 %all-gather.4.cloned.1.call-done = bf16[1280,1152]{1,0:T(8,128)(2,1)} async-done(((bf16[320,1152]{1,0:T(8,128)(2,1)}), bf16[1280,1152]{1,0:T(8,128)(2,1)}) %all-gather.4.cloned.1.call-update) | async-done | bytes 2949136 | tf_op jit(solution)/shard_map/all_gather | solution.py:48
  141.8 0.0 copy-done.2
  141.8 4.6 %fusion.2 = bf16[1,448,1280]{2,1,0:T(8,128)(2,1)} fusion(bf16[1280,1152]{1,0:T(8,128)(2,1)} %all-gather.4.cloned.1.call-done, bf16[1,448,1152]{2,1,0:T(8,128)(2,1)S(1)} %copy-done.2, pred[448]{0:T(512)(128)(4,1)S(1)} %add_compare_fusion), kind=kOutput, calls=%fused_computation.6 | convolution fusion | flops 1322295296 | bytes 5128640 | tf_op jit(solution)/shard_map/dot_general | solution.py:46
  146.3 23.1 %all-gather.6.cloned.1.call-done = bf16[1280,1152]{1,0:T(8,128)(2,1)} async-done(((bf16[320,1152]{1,0:T(8,128)(2,1)}), bf16[1280,1152]{1,0:T(8,128)(2,1)}) %all-gather.6.cloned.1.call-update) | async-done | bytes 2949136 | tf_op jit(solution)/shard_map/all_gather | solution.py:62
  169.4 4.5 %reshape.31 = bf16[4,368640]{1,0:T(4,128)(2,1)} reshape(bf16[1280,1152]{1,0:T(8,128)(2,1)} %all-gather.6.cloned.1.call-done) | data formatting | bytes 5898240 | tf_op jit(solution)/shard_map/reshape | solution.py:64
  173.9 12.6 %fusion = bf16[16,368640]{1,0:T(8,128)(2,1)S(1)} fusion(bf16[4,368640]{1,0:T(4,128)(2,1)} %reshape.31, f32[4,32]{1,0:T(4,128)S(1)} %fusion.11, s32[]{:T(128)S(6)} %select_n.28), kind=kOutput, calls=%fused_computation.1 | convolution fusion | flops 294912000 | bytes 14746116 | tf_op jit(solution)/shard_map/dot_general | solution.py:65
  186.5 0.0 copy-start.1
  186.6 5.3 %copy.13 = bf16[2,8,320,1152]{3,2,1,0:T(8,128)(2,1)} copy(bf16[2,8,320,1152]{3,1,2,0:T(8,128)(2,1)S(1)} %bitcast.21) | data formatting | bytes 23592960
  191.8 0.0 copy-done.1
Async XLA Ops:
  7.2 2.1 %copy-start = (bf16[1,448,1280]{2,1,0:T(8,128)(2,1)S(1)}, bf16[1,448,1280]{2,1,0:T(8,128)(2,1)}, u32[]{:S(2)}) copy-start(bf16[1,448,1280]{2,1,0:T(8,128)(2,1)} %param.6) | copy-start | bytes 3440644
  7.2 72.5 %reduce-scatter.4.cloned.1.call-start = ((), (), s32[]{:S(2)}) async-start(), calls=%async_computation.4 | async-start | bytes 3686400 | tf_op jit(solution)/shard_map/reduce_scatter | solution.py:53
  19.4 122.4 %all-gather.4.cloned.1.call-start = ((), (), s32[]{:S(2)}) async-start(), calls=%async_computation.2 | async-start | bytes 3686400 | tf_op jit(solution)/shard_map/all_gather | solution.py:48
  19.5 13.7 %copy-start.3 = (f32[16,32]{1,0:T(8,128)S(1)}, f32[16,32]{1,0:T(8,128)}, u32[]{:S(2)}) copy-start(f32[16,32]{1,0:T(8,128)} %param.9) | copy-start | bytes 6148
  19.5 13.7 %copy-start.4 = (s32[4]{0:T(128)S(1)}, s32[4]{0:T(128)}, u32[]{:S(2)}) copy-start(s32[4]{0:T(128)} %param.10) | copy-start | bytes 52
  46.8 94.9 %copy-start.2 = (bf16[1,448,1152]{2,1,0:T(8,128)(2,1)S(1)}, bf16[1,448,1152]{2,1,0:T(8,128)(2,1)}, u32[]{:S(2)}) copy-start(bf16[1,448,1152]{2,1,0:T(8,128)(2,1)} %param.7) | copy-start | bytes 3096580
  70.5 98.9 %all-gather.6.cloned.1.call-start = ((), (), s32[]{:S(2)}) async-start(), calls=%async_computation.3 | async-start | bytes 3686400 | tf_op jit(solution)/shard_map/all_gather | solution.py:62
  186.5 5.3 %copy-start.1 = (bf16[1,448,1280]{2,1,0:T(8,128)(2,1)S(1)}, bf16[1,448,1280]{2,1,0:T(8,128)(2,1)}, u32[]{:S(2)}) copy-start(bf16[1,448,1280]{2,1,0:T(8,128)(2,1)} %param.6) | copy-start | bytes 3440644
Sparse Core Ops, SparseCore 0:
  19.5 60.0 reduce-scatter.3
  81.8 59.9 all-gather.3
  143.3 26.0 all-gather.5
where the time goes:
time: 199 us; the launch traced here: 198 us
  waiting for transfers between devices  94.3 us (47%)
  other arithmetic  30.4 us (15%)
  blocking collectives  22.3 us (11%)
  matrix products  22 us (11%)
  local copies, waits for them, and re-layouts  15.3 us (8%)
  between operations  13.8 us (7%)
    all_gather x1, waiting for transfers between devices, body(): lax.all_gather(merged_rows, 'edge', axis=0, tiled=True)  62.1 us
    all_gather x1, waiting for transfers between devices, body(): lax.all_gather(system_rows[None], ('expert', 'sys'), axis=0, tiled=True)  23.1 us
    all_to_all x1, blocking collectives, body(): lax.all_to_all(partials, 'expert', split_axis=0, concat_axis=0, tiled=True)  22.3 us
    convert_element_type x1, other arithmetic, body(): expert_weights.astype(jnp.float32)[None]  13.6 us
    reduce_sum x1, other arithmetic, body(): jnp.sum(own_coeffs[:, :, None, None] * expert_weights.astype(jnp.float32)...  13.5 us
    dot_general x1, matrix products, body(): folded = jnp.dot(local_coeffs, flat_rows, precision=highest)  12.6 us
    unnamed x12, local copies, waits for them, and re-layouts  10.7 us
    reduce_scatter x1, waiting for transfers between devices, body(): lax.psum_scatter(lax.dot_general(features, masked_grad, (((0,), (0,)), ((...  9.04 us
  transfers between devices with their start and end apart: 3, of which 3 were waited for; matrix products, arithmetic and copies ran while one was open for 17% of the time, Pallas kernels for 0%

commit v1 on v0

--- a/solution.py
+++ b/solution.py
@@ -59,7 +59,23 @@
         tiled=True,
     )
     local_coeffs = lax.dynamic_slice_in_dim(coeffs, expert_at * exp_local, exp_local, 1).T
-    block_rows = lax.all_gather(system_rows[None], ("expert", "sys"), axis=0, tiled=True)
+    devices, index, rows = (
+        lax.axis_size(("expert", "sys")),
+        lax.axis_index(("expert", "sys")),
+        system_rows[None].shape[0],
+    )
+    ahead = [(i, (i + 1) % devices) for i in range(devices)]
+    out = jnp.zeros(
+        (*system_rows[None].shape[:0], devices * rows, *system_rows[None].shape[0 + 1 :]),
+        system_rows[None].dtype,
+    )
+    held = system_rows[None]
+    for lap in range(devices):
+        owner = (index - lap) % devices
+        out = lax.dynamic_update_slice_in_dim(out, held, owner * rows, axis=0)
+        if lap < devices - 1:
+            held = lax.ppermute(held, ("expert", "sys"), ahead)
+    block_rows = out
     span_rows = block_rows.shape[0]
     flat_rows = block_rows.reshape(span_rows, -1).astype(jnp.float32)
     folded = jnp.dot(local_coeffs, flat_rows, precision=highest)

time: 199 us -> 184 us (0.925)
  waiting for transfers between devices: 94.3 us -> 79.2 us
    all_gather x1 -> x0, waiting for transfers between devices: 23.1 us -> none  [body(): lax.all_gather(system_rows[None], ('expert', 'sys'), axis=0, tiled=True)]
    ppermute x0 -> x3, waiting for transfers between devices: none -> 21.2 us  [body(): held = lax.ppermute(held, ('expert', 'sys'), ahead)]
    all_gather x1, waiting for transfers between devices: 62.1 us -> 48.6 us  [body(): lax.all_gather(merged_rows, 'edge', axis=0, tiled=True)]
    unnamed x3, waiting for transfers between devices: 0.05 us -> 9.34 us
    reduce_scatter x1 -> x0, waiting for transfers between devices: 9.04 us -> none  [body(): lax.psum_scatter(lax.dot_general(features, masked_grad, (((0,), (0,)), ((...]
    reshape x1 -> x0, local copies, waits for them, and re-layouts: 4.52 us -> none  [body(): flat_rows = block_rows.reshape(span_rows, -1).astype(jnp.float32)]
    unnamed x12, local copies, waits for them, and re-layouts: 10.7 us -> 14.7 us
  transfers between devices with their start and end apart: 3 -> 5, of which waited for: 3 -> 4; matrix products, arithmetic and copies ran while one was open for 17% -> 20% of each run, Pallas kernels for 0% -> 0%
where the time goes in v1:
time: 184 us; the launch traced here: 183 us
  waiting for transfers between devices  79.2 us (43%)
  other arithmetic  30.4 us (17%)
  blocking collectives  22.2 us (12%)
  matrix products  20.9 us (11%)
  local copies, waits for them, and re-layouts  16.2 us (9%)
  between operations  14.2 us (8%)
    all_gather x1, waiting for transfers between devices, body(): lax.all_gather(merged_rows, 'edge', axis=0, tiled=True)  48.6 us
    all_to_all x1, blocking collectives, body(): lax.all_to_all(partials, 'expert', split_axis=0, concat_axis=0, tiled=True)  22.2 us
    ppermute x3, waiting for transfers between devices, body(): held = lax.ppermute(held, ('expert', 'sys'), ahead)  21.2 us
    unnamed x12, local copies, waits for them, and re-layouts  14.7 us
    convert_element_type x1, other arithmetic, body(): expert_weights.astype(jnp.float32)[None]  13.6 us
    reduce_sum x1, other arithmetic, body(): jnp.sum(own_coeffs[:, :, None, None] * expert_weights.astype(jnp.float32)...  13.5 us
    dot_general x1, matrix products, body(): folded = jnp.dot(local_coeffs, flat_rows, precision=highest)  11.2 us
    unnamed x3, waiting for transfers between devices  9.34 us
  transfers between devices with their start and end apart: 5, of which 4 were waited for; matrix products, arithmetic and copies ran while one was open for 20% of the time, Pallas kernels for 0%

profile of v1, /device:TPU:0, one launch (start us, length us, event | category | flops | bytes accessed | tf_op | source)
XLA Modules:
  0.0 183.2 jit_solution(4136641017780971516)
XLA Ops:
  7.2 0.0 copy-start
  7.2 0.0 reduce-scatter.4.cloned.1.call-start
  7.2 1.4 fusion.14
  8.6 0.7 add_compare_fusion
  9.3 0.0 copy-done
  9.3 4.6 %fusion.1 = bf16[1280,1152]{0,1:T(8,128)(2,1)} fusion(bf16[1,448,1280]{2,1,0:T(8,128)(2,1)S(1)} %copy-done, bf16[1,448,1152]{2,1,0:T(8,128)(2,1)} %param.7, pred[448]{0:T(512)(128)(4,1)S(1)} %add_compare_fusion), kind=kOutput, calls=%fused_computation.4 | convolution fusion | flops 1323196416 | bytes 5128640 | tf_op jit(solution)/shard_map/dot_general | solution.py:54
  13.9 5.4 %copy.16 = bf16[1280,1152]{1,0:T(8,128)(2,1)} copy(bf16[1280,1152]{0,1:T(8,128)(2,1)} %fusion.1) | data formatting | bytes 5898240
  19.4 0.0 reduce-scatter.4.cloned.1.call-update
  19.4 0.0 all-gather.2.cloned.1.call-start
  19.4 0.0 copy-start.2
  19.5 0.0 copy-start.3
  19.5 13.6 %convert_element_type.25 = f32[16,320,1152]{2,1,0:T(8,128)} convert(bf16[16,320,1152]{2,1,0:T(8,128)(2,1)} %param.8) | non-fusion elementwise | flops 5898240 | bytes 35389440 | tf_op jit(solution)/shard_map/convert_element_type | solution.py:38
  33.1 0.0 copy-done.2
  33.1 0.0 copy-done.3
  33.1 0.2 fusion.11
  33.3 0.1 constant_dynamic-slice_fusion
  33.3 13.5 %multiply_reduce_fusion = bf16[2,320,1152]{2,1,0:T(8,128)(2,1)S(1)} fusion(f32[16,320,1152]{2,1,0:T(8,128)} %convert_element_type.25, f32[2,16]{1,0:T(2,128)S(1)} %bitcast.30), kind=kLoop, calls=%fused_computation.2 | loop fusion | flops 22855680 | bytes 25067648 | tf_op jit(solution)/shard_map/reduce_sum | solution.py:37
  46.8 22.2 %all_to_all.5 = bf16[2,320,1152]{2,1,0:T(8,128)(2,1)S(1)} all-to-all(bf16[2,320,1152]{2,1,0:T(8,128)(2,1)S(1)} %multiply_reduce_fusion), channel_id=1, replica_groups=mesh['groups'=2,'edge'=4,'expert'=2,'sys'=2] {'expert'}, dimensions={0} | all-to-all | bytes 2949120 | tf_op jit(solution)/shard_map/all_to_all | solution.py:41
  69.0 1.3 reduce_sum.32
  70.3 0.0 all-gather.2.cloned.1.call-update
  70.3 9.3 %reduce-scatter.4.cloned.1.call-done = bf16[320,1152]{1,0:T(8,128)(2,1)} async-done(((bf16[1280,1152]{1,0:T(8,128)(2,1)}), bf16[320,1152]{1,0:T(8,128)(2,1)}) %reduce-scatter.4.cloned.1.call-update) | async-done | bytes 737296
  79.6 1.7 copy.17
  81.4 0.8 copy.14
  82.2 0.1 collective-permute-start
  82.3 10.9 %collective-permute-done = bf16[1,320,1152]{2,1,0:T(8,128)(2,1)S(1)} collective-permute-done((bf16[1,320,1152]{2,1,0:T(8,128)(2,1)S(1)}, bf16[1,320,1152]{2,1,0:T(8,128)(2,1)S(1)}, u32[]{:S(2)}, u32[]{:S(2)}) %collective-permute-start) | collective-permute-done | bytes 737312 | tf_op jit(solution)/shard_map/ppermute | solution.py:77
  93.1 0.0 collective-permute-start.1
  93.1 48.6 %all-gather.2.cloned.1.call-done = bf16[1280,1152]{1,0:T(8,128)(2,1)} async-done(((bf16[320,1152]{1,0:T(8,128)(2,1)}), bf16[1280,1152]{1,0:T(8,128)(2,1)}) %all-gather.2.cloned.1.call-update) | async-done | bytes 2949136 | tf_op jit(solution)/shard_map/all_gather | solution.py:48
  141.8 4.9 %fusion.2 = bf16[1,448,1280]{2,1,0:T(8,128)(2,1)} fusion(bf16[1280,1152]{1,0:T(8,128)(2,1)} %all-gather.2.cloned.1.call-done, bf16[1,448,1152]{2,1,0:T(8,128)(2,1)} %param.7, pred[448]{0:T(512)(128)(4,1)S(1)} %add_compare_fusion), kind=kOutput, calls=%fused_computation.6 | convolution fusion | flops 1322295296 | bytes 5128640 | tf_op jit(solution)/shard_map/dot_general | solution.py:46
  146.6 0.0 collective-permute-done.1
  146.6 0.0 collective-permute-start.2
  146.6 0.2 broadcast_in_dim.38
  146.9 0.1 constant_dynamic-update-slice_fusion.3
  147.0 0.1 constant_dynamic-update-slice_fusion.2
  147.1 0.1 constant_dynamic-update-slice_fusion.1
  147.2 10.3 %collective-permute-done.2 = bf16[1,320,1152]{2,1,0:T(8,128)(2,1)S(1)} collective-permute-done((bf16[1,320,1152]{2,1,0:T(8,128)(2,1)S(1)}, bf16[1,320,1152]{2,1,0:T(8,128)(2,1)S(1)}, u32[]{:S(2)}, u32[]{:S(2)}) %collective-permute-start.2) | collective-permute-done | bytes 737312 | tf_op jit(solution)/shard_map/ppermute | solution.py:77
  157.5 0.1 constant_dynamic-update-slice_fusion
  157.6 2.3 %copy.18 = bf16[1,4,320,1152]{3,1,2,0:T(4,128)(2,1)S(1)} copy(bf16[1,4,320,1152]{3,2,1,0:T(8,128)(2,1)S(1)} %bitcast.27) | data formatting | bytes 5898240
  159.9 11.2 %fusion = bf16[16,368640]{1,0:T(8,128)(2,1)S(1)} fusion(bf16[4,368640]{1,0:T(4,128)(2,1)S(1)} %bitcast.25, f32[4,32]{1,0:T(4,128)S(1)} %fusion.11, s32[]{:T(128)S(6)} %select_n.59), kind=kOutput, calls=%fused_computation.1 | convolution fusion | flops 294912000 | bytes 14746116 | tf_op jit(solution)/shard_map/dot_general | solution.py:81
  171.1 0.0 copy-start.1
  171.1 5.3 %copy.19 = bf16[2,8,320,1152]{3,2,1,0:T(8,128)(2,1)} copy(bf16[2,8,320,1152]{3,1,2,0:T(8,128)(2,1)S(1)} %bitcast.24) | data formatting | bytes 23592960
  176.3 0.0 copy-done.1
Async XLA Ops:
  7.2 2.1 %copy-start = (bf16[1,448,1280]{2,1,0:T(8,128)(2,1)S(1)}, bf16[1,448,1280]{2,1,0:T(8,128)(2,1)}, u32[]{:S(2)}) copy-start(bf16[1,448,1280]{2,1,0:T(8,128)(2,1)} %param.6) | copy-start | bytes 3440644
  7.2 72.5 %reduce-scatter.4.cloned.1.call-start = ((), (), s32[]{:S(2)}) async-start(), calls=%async_computation.3 | async-start | bytes 3686400
  19.4 122.4 %all-gather.2.cloned.1.call-start = ((), (), s32[]{:S(2)}) async-start(), calls=%async_computation.2 | async-start | bytes 3686400 | tf_op jit(solution)/shard_map/all_gather | solution.py:48
  19.4 13.6 %copy-start.2 = (f32[16,32]{1,0:T(8,128)S(1)}, f32[16,32]{1,0:T(8,128)}, u32[]{:S(2)}) copy-start(f32[16,32]{1,0:T(8,128)} %param.9) | copy-start | bytes 6148
  19.5 13.6 %copy-start.3 = (s32[4]{0:T(128)S(1)}, s32[4]{0:T(128)}, u32[]{:S(2)}) copy-start(s32[4]{0:T(128)} %param.10) | copy-start | bytes 52
  82.2 10.9 %collective-permute-start = (bf16[1,320,1152]{2,1,0:T(8,128)(2,1)S(1)}, bf16[1,320,1152]{2,1,0:T(8,128)(2,1)S(1)}, u32[]{:S(2)}, u32[]{:S(2)}) collective-permute-start(bf16[1,320,1152]{2,1,0:T(8,128)(2,1)S(1)} %copy.14), channel_id=1, source_target_pairs={{0,1},{1,2},{2,3},{3,0},{4,5},{5,6},{6,7},{7,4},{8,9},{9,10},{10,1... | collective-permute-start | bytes 2211848 | tf_op jit(solution)/shard_map/ppermute | solution.py:77
  93.1 53.5 %collective-permute-start.1 = (bf16[1,320,1152]{2,1,0:T(8,128)(2,1)S(1)}, bf16[1,320,1152]{2,1,0:T(8,128)(2,1)S(1)}, u32[]{:S(2)}, u32[]{:S(2)}) collective-permute-start(bf16[1,320,1152]{2,1,0:T(8,128)(2,1)S(1)} %collective-permute-done), channel_id=1, source_target_pairs={{0,1},{1,2},{2,3},{3,0},{4,5},{5,6},{6,7},{7,4},{8,9},{9,10},{10,1... | collective-permute-start | bytes 2211848 | tf_op jit(solution)/shard_map/ppermute | solution.py:77
  146.6 10.9 %collective-permute-start.2 = (bf16[1,320,1152]{2,1,0:T(8,128)(2,1)S(1)}, bf16[1,320,1152]{2,1,0:T(8,128)(2,1)S(1)}, u32[]{:S(2)}, u32[]{:S(2)}) collective-permute-start(bf16[1,320,1152]{2,1,0:T(8,128)(2,1)S(1)} %collective-permute-done.1), channel_id=1, source_target_pairs={{0,1},{1,2},{2,3},{3,0},{4,5},{5,6},{6,7},{7,4},{8,9},{9,10},{10,1... | collective-permute-start | bytes 2211848 | tf_op jit(solution)/shard_map/ppermute | solution.py:77
  171.1 5.3 %copy-start.1 = (bf16[1,448,1280]{2,1,0:T(8,128)(2,1)S(1)}, bf16[1,448,1280]{2,1,0:T(8,128)(2,1)}, u32[]{:S(2)}) copy-start(bf16[1,448,1280]{2,1,0:T(8,128)(2,1)} %param.6) | copy-start | bytes 3440644
Sparse Core Ops, SparseCore 0:
  19.5 60.0 reduce-scatter.3
  81.8 59.9 all-gather.1
